TPU v7x, 32 devices: a whole 2x2x4 slice. The times are simulated.
32 devices in a mesh: cfg: 2 (over x), work: 16 (over z, y, core).
Axes of the slice: x: 2, y: 2, z: 4, core: 2. Of those that a mesh axis runs over, the one named last changes fastest.
Arguments:
- sources: bfloat16 [32, 16384, 128], P('cfg', 'work'), parts along dimension 0, may hold values from -6 to 6
- perambs: bfloat16 [192, 16384], P('cfg', 'work'), parts along dimension 0, may hold values from -0.5 to 0.5
- source_ids: int32 [16], replicated, may hold values from 0 to 15
- peramb_ids: int32 [48, 3], replicated, may hold values from 0 to 95
- sink_counts: int32 [16], replicated, may hold values from 1 to 6, 48 in all
- weights: float32 [48], replicated, may hold values from -2 to 2, as said below
Outputs:
- sink_tensors: bfloat16 [32, 16384, 128], P(('cfg', 'work')), parts along dimension 0
There are 2 independent parts, one for each index of `cfg`. A program takes and returns all parts, laid end to end along the dimension named above; an argument that names none is the same for every part. Nothing has to cross between parts.
Inputs may be any that keep to these rules, and one draw needn't show every extreme that they name: `sink_counts`: diagrams are listed sink by sink in order; the counts add up to 48 and some sink has exactly 6 diagrams. `weights`: nonzero multiples of 1/4.
All inputs are finite; a program needn't handle non-finite values.
Results may differ from a plain program's by a relative error of at most 0.0064.
Values may be sent and summed in bfloat16 or wider, within the bound.
A program may use at most 128 MiB of HBM per device.

v0:
```python
import functools

import jax
import jax.numpy as jnp
import numpy as np
from jax import lax
from jax.experimental import pallas as pl
from jax.experimental.pallas import tpu as pltpu
from jax.sharding import PartitionSpec as P

MOST = 6
LEGS = 3
PAD = 8
MESH = pl.DeviceIdType.MESH


def pick_kernel(
    ids_ref, legs_ids_ref, counts_ref, x_ref, p_ref, o_ref, l_ref, rows, sem
):
    sinks = o_ref.shape[0]
    diagrams = legs_ids_ref.shape[1]
    own_rows, extent = l_ref.shape[2], l_ref.shape[3]

    @pl.loop(0, sinks)
    def _(s):
        pltpu.make_async_copy(x_ref.at[ids_ref[s]], o_ref.at[s], sem.at[s]).start()

    for r in range(own_rows):
        rows[:, r, :] = p_ref[:, r * extent : (r + 1) * extent].astype(jnp.float32)

    def one(s, start):
        for slot in range(MOST):
            d = jnp.minimum(start + slot, diagrams - 1)
            for leg in range(LEGS):
                l_ref[s, slot * LEGS + leg] = rows[legs_ids_ref[leg, d]].astype(
                    jnp.bfloat16
                )
        return start + counts_ref[s]

    lax.fori_loop(0, sinks, one, jnp.int32(0))

    @pl.loop(0, sinks)
    def _(s):
        pltpu.make_async_copy(x_ref.at[0], o_ref.at[s], sem.at[s]).wait()


def pick(sources, perambs, source_ids, leg_ids, counts):
    sinks = source_ids.shape[0]
    own_rows, extent = sources.shape[1], sources.shape[3]
    smem = pl.BlockSpec(memory_space=pltpu.SMEM)
    return pl.pallas_call(
        pick_kernel,
        out_shape=(
            jax.ShapeDtypeStruct((sinks,) + sources.shape[1:], sources.dtype),
            jax.ShapeDtypeStruct((sinks, MOST * LEGS, own_rows, extent), perambs.dtype),
        ),
        in_specs=[
            smem,
            smem,
            smem,
            pl.BlockSpec(memory_space=pl.ANY),
            pl.BlockSpec(memory_space=pltpu.VMEM),
        ],
        out_specs=(
            pl.BlockSpec(memory_space=pltpu.VMEM),
            pl.BlockSpec(memory_space=pltpu.VMEM),
        ),
        scratch_shapes=[
            pltpu.VMEM((perambs.shape[0], own_rows, extent), jnp.float32),
            pltpu.SemaphoreType.DMA((sinks,)),
        ],
        compiler_params=pltpu.CompilerParams(vmem_limit_bytes=12 * 1024 * 1024),
        name="pick",
    )(source_ids, leg_ids, counts, sources, perambs)


def split_rows(own_a):
    sizes, left = [], own_a
    while left > 0:
        sizes.append(2 if left > 2 else 1)
        left -= sizes[-1]
    return sizes


def contract_kernel(
    workers,
    counts_ref,
    weights_ref,
    key_ref,
    x_ref,
    legs_ref,
    o_ref,
    xbuf,
    lbuf,
    legs,
    p1s,
    p2s,
    p3s,
    mid,
    acc,
    stage,
    own_sem,
    xsend,
    xrecv,
    lsend,
    lrecv,
):
    own_a, extent = xbuf.shape[0], xbuf.shape[2]
    diagrams = weights_ref.shape[0]
    sizes = split_rows(own_a)
    step = extent + PAD
    me = lax.axis_index("work")

    def leg_copy(t):
        peer = lax.rem(me + t, workers)
        return pltpu.make_async_remote_copy(
            src_ref=legs_ref.at[peer],
            dst_ref=lbuf.at[me],
            send_sem=lsend.at[t],
            recv_sem=lrecv.at[t],
            device_id={"work": peer},
            device_id_type=MESH,
        )

    def x_copy(j, t):
        peer = lax.rem(me + t, workers)
        return pltpu.make_async_remote_copy(
            src_ref=x_ref.at[peer, j],
            dst_ref=xbuf.at[j, me],
            send_sem=xsend.at[j, t],
            recv_sem=xrecv.at[j, t],
            device_id={"work": peer},
            device_id_type=MESH,
        )

    own = [
        pltpu.make_async_copy(x_ref.at[me, j], xbuf.at[j, me], own_sem.at[j])
        for j in range(own_a)
    ]
    own.append(pltpu.make_async_copy(legs_ref.at[me], lbuf.at[me], own_sem.at[own_a]))
    for copy in own:
        copy.start()

    barrier = pltpu.get_barrier_semaphore()

    @pl.loop(1, workers)
    def _(t):
        peer = lax.rem(me + t, workers)
        pl.semaphore_signal(barrier, inc=1, device_id={"work": peer}, device_id_type=MESH)

    pl.semaphore_wait(barrier, workers - 1)

    @pl.loop(1, workers)
    def _(t):
        leg_copy(t).start()

    @pl.loop(0, own_a)
    def _(j):
        @pl.loop(1, workers)
        def _(t):
            x_copy(j, t).start()

    start = lax.fori_loop(
        0, workers, lambda s, v: v + jnp.where(s < me, counts_ref[s], 0), jnp.int32(0)
    )
    factors = []
    for d in range(MOST):
        value = weights_ref[jnp.minimum(start + d, diagrams - 1)]
        factors.append(jnp.where(d < counts_ref[me], value, 0.0))

    own[own_a].wait()

    @pl.loop(1, workers)
    def _(t):
        leg_copy(t).wait()

    own_rows = lbuf.shape[2]

    @pl.loop(0, MOST * LEGS)
    def _(m):
        for v in range(workers):
            legs[m, v * own_rows : (v + 1) * own_rows, :] = lbuf[v, m].astype(jnp.float32)

    firsts = []
    for d in range(MOST):
        firsts.append(legs[LEGS * d].astype(jnp.bfloat16))
        p2s[d * extent : (d + 1) * extent, :] = legs[LEGS * d + 1].astype(jnp.bfloat16)
        p3s[d] = legs[LEGS * d + 2].T.astype(jnp.bfloat16)
    side = jnp.concatenate(firsts, axis=1)
    low = 0
    for c, size in enumerate(sizes):
        width = MOST * size * workers
        rows = lax.broadcasted_iota(jnp.int32, (MOST * extent, width), 0)
        chosen = jnp.where(rows == key_ref[c, :, :width], 1.0, 0.0).astype(jnp.bfloat16)
        p1s[c, :, :width] = jnp.dot(side, chosen, preferred_element_type=jnp.float32).astype(
            jnp.bfloat16
        )

    group = 4
    wide = 8
    for c, size in enumerate(sizes):
        count = size * workers
        for j in range(low, low + size):
            own[j].wait()

            @pl.loop(1, workers)
            def _(t):
                x_copy(j, t).wait()

        @pl.loop(0, count // group, unroll=2)
        def _(g):
            j = low + lax.div(g * group, workers)
            v = lax.rem(g * group, workers)
            both = jnp.concatenate([xbuf[j, v + i] for i in range(group)], axis=1)
            for d in range(MOST):
                z = jnp.dot(
                    p2s[d * extent : (d + 1) * extent, :], both, preferred_element_type=jnp.float32
                ).astype(jnp.bfloat16)
                stacked = jnp.concatenate(
                    [z[:, i * extent : (i + 1) * extent] for i in range(group)], axis=0
                )
                y = jnp.dot(stacked, p3s[d], preferred_element_type=jnp.float32) * factors[d]
                for i in range(group):
                    at = pl.multiple_of((d * count + group * g + i) * step, 8)
                    mid[pl.ds(at, extent), :] = y[i * extent : (i + 1) * extent]

        low += size

        def pieces(b):
            cols = [
                mid[pl.ds(wide * b + h, MOST * count, stride=step), :].astype(jnp.bfloat16)
                for h in range(wide)
            ]
            t = jnp.dot(
                p1s[c, :, : MOST * count],
                jnp.concatenate(cols, axis=1),
                preferred_element_type=jnp.float32,
            )
            out = []
            for h in range(wide):
                at = pl.ds(pl.multiple_of((wide * b + h) * extent, 8), extent)
                piece = t[:, h * extent : (h + 1) * extent]
                out.append((at, piece if c == 0 else piece + acc[at, :]))
            return out

        if c < len(sizes) - 1:

            @pl.loop(0, extent // wide)
            def _(b):
                for at, piece in pieces(b):
                    acc[at, :] = piece

        else:

            @pl.loop(0, extent // (2 * wide))
            def _(b):
                for half in range(2):
                    for h, (at, piece) in enumerate(pieces(2 * b + half)):
                        stage[:, half * wide + h, :] = piece
                at = pl.ds(pl.multiple_of(2 * wide * b, 2 * wide), 2 * wide)
                o_ref[:, at, :] = stage[:, : 2 * wide, :].astype(jnp.bfloat16)


def contract(x, legs, counts, weights, workers):
    own_a, extent = x.shape[1], x.shape[2]
    sizes = split_rows(own_a)
    most = max(sizes) * workers
    keys = np.full((len(sizes), 1, MOST * most), -1)
    low = 0
    for c, size in enumerate(sizes):
        count = size * workers
        col = np.arange(MOST * count)
        at = col % count
        keys[c, 0, : MOST * count] = (
            col // count * extent + at % workers * own_a + low + at // workers
        )
        low += size
    step = extent + PAD
    smem = pl.BlockSpec(memory_space=pltpu.SMEM)
    return pl.pallas_call(
        functools.partial(contract_kernel, workers),
        out_shape=jax.ShapeDtypeStruct((extent, extent, extent), jnp.bfloat16),
        in_specs=[
            smem,
            smem,
            pl.BlockSpec(memory_space=pltpu.VMEM),
            pl.BlockSpec(memory_space=pl.ANY),
            pl.BlockSpec(memory_space=pl.ANY),
        ],
        out_specs=pl.BlockSpec(memory_space=pltpu.VMEM),
        scratch_shapes=[
            pltpu.VMEM((own_a, workers, extent, extent), jnp.bfloat16),
            pltpu.VMEM((workers,) + legs.shape[1:], jnp.bfloat16),
            pltpu.VMEM((MOST * LEGS, extent, extent), jnp.float32),
            pltpu.VMEM((len(sizes), extent, MOST * most), jnp.bfloat16),
            pltpu.VMEM((MOST * extent, extent), jnp.bfloat16),
            pltpu.VMEM((MOST, extent, extent), jnp.bfloat16),
            pltpu.VMEM((MOST * most * step, extent), jnp.float32),
            pltpu.VMEM((extent * extent, extent), jnp.float32),
            pltpu.VMEM((extent, 24, extent), jnp.float32),
            pltpu.SemaphoreType.DMA((own_a + 1,)),
            pltpu.SemaphoreType.DMA((own_a, workers)),
            pltpu.SemaphoreType.DMA((own_a, workers)),
            pltpu.SemaphoreType.DMA((workers,)),
            pltpu.SemaphoreType.DMA((workers,)),
        ],
        compiler_params=pltpu.CompilerParams(
            vmem_limit_bytes=MOST * most * step * extent * 4 + 26 * 1024 * 1024, collective_id=0, has_side_effects=True
        ),
        name="contract",
    )(counts, weights, jnp.asarray(keys, jnp.int32), x, legs)


def per_device(sources, perambs, source_ids, peramb_ids, sink_counts, weights):
    workers = lax.axis_size("work")
    extent = sources.shape[2]
    own_a = sources.shape[1] // extent
    picked, legs = pick(
        sources.reshape(-1, own_a, extent, extent),
        perambs,
        source_ids,
        peramb_ids.T,
        sink_counts,
    )
    total = contract(picked, legs, sink_counts, weights, workers)
    return total.reshape(1, extent * extent, extent)


def solution(mesh):
    return jax.shard_map(
        per_device,
        mesh=mesh,
        in_specs=(P("cfg", "work", None), P("cfg", "work"), P(), P(), P(), P()),
        out_specs=P(("cfg", "work"), None, None),
        check_vma=False,
    )
```

profile of v0, /device:TPU:0, one launch (start us, length us, event | category | flops | bytes accessed | tf_op | source)
XLA Modules:
  0.0 131.1 jit_solution(17629030763999030048)
XLA Ops:
  0.0 0.0 copy-start.5
  0.0 0.0 copy-start.7
  0.0 0.0 copy-start
  0.0 2.2 %copy-done = bf16[16,1024,128]{2,1,0:T(8,128)(2,1)S(1)} copy-done((bf16[16,1024,128]{2,1,0:T(8,128)(2,1)S(1)}, bf16[16,1024,128]{2,1,0:T(8,128)(2,1)}, u32[]{:S(2)}) %copy-start) | copy-done | bytes 4194328
  2.2 0.0 copy-start.1
  2.2 0.9 copy-done.1
  3.1 0.0 copy-start.3
  3.1 0.7 copy-done.3
  3.8 0.0 copy-start.4
  3.8 0.7 copy-done.4
  4.5 0.0 copy-start.6
  4.5 0.7 copy-done.6
  5.1 0.0 copy-start.2
  5.1 2.1 %pick.1 = (bf16[16,8,128,128]{3,2,1,0:T(8,128)(2,1)S(1)}, bf16[16,18,8,128]{3,2,1,0:T(8,128)(2,1)S(1)}) custom-call(s32[16]{0:T(128)S(1)} %copy-done.6, s32[3,48]{1,0:T(4,128)S(1)} %bitcast.5, s32[16]{0:T(128)S(1)} %copy-done.4, bf16[16,8,128,128]{3,2,1,0:T(8,128)(2,1)S(1)} %bitcast.4, bf16[96,1024]{1,0:T(8,128)(2,1)S(1)} %copy-done.1), custom_call_target="tpu_custom_call" | custom-call | tf_op jit(solution)/shard_map/pick/pallas_call | solution.py:51
  7.2 0.0 copy-done.5
  7.2 0.0 copy-done.7
  7.2 0.0 copy-done.2
  7.2 121.9 %contract.1 = bf16[128,128,128]{2,1,0:T(8,128)(2,1)S(1)} custom-call(s32[16]{0:T(128)S(1)} %copy-done.5, f32[48]{0:T(128)S(1)} %copy-done.7, s32[5,1,192]{2,1,0:T(1,128)S(1)} %copy-done.2, bf16[16,8,128,128]{3,2,1,0:T(8,128)(2,1)S(1)} %get-tuple-element.7.x_ref, bf16[16,18,8,128]{3,2,1,0:T(8,128)(2,1)S(1)} %get-tuple-element.8.legs_ref), custom_call_target="tpu_custom_call" | custom-call | tf_op jit(solution)/shard_map/contract/pallas_call | solution.py:280
  129.1 2.0 %copy.9 = bf16[1,16384,128]{2,1,0:T(8,128)(2,1)} copy(bf16[1,16384,128]{2,1,0:T(8,128)(2,1)S(1)} %bitcast.3) | data formatting | bytes 8388608
Async XLA Ops:
  0.0 7.2 %copy-start.5 = (s32[16]{0:T(128)S(1)}, s32[16]{0:T(128)}, u32[]{:S(2)}) copy-start(s32[16]{0:T(128)} %counts_ref.3) | copy-start | bytes 196
  0.0 7.2 %copy-start.7 = (f32[48]{0:T(128)S(1)}, f32[48]{0:T(128)}, u32[]{:S(2)}) copy-start(f32[48]{0:T(128)} %weights_ref.1) | copy-start | bytes 580
  0.0 2.2 %copy-start = (bf16[16,1024,128]{2,1,0:T(8,128)(2,1)S(1)}, bf16[16,1024,128]{2,1,0:T(8,128)(2,1)}, u32[]{:S(2)}) copy-start(bf16[16,1024,128]{2,1,0:T(8,128)(2,1)} %param.7) | copy-start | bytes 12582916
  2.2 0.9 copy-start.1
  3.1 0.7 copy-start.3
  3.8 0.7 copy-start.4
  4.5 0.7 copy-start.6
  5.1 2.1 %copy-start.2 = (s32[5,1,192]{2,1,0:T(1,128)S(1)}, s32[5,1,192]{2,1,0:T(1,128)}, u32[]{:S(2)}) copy-start(s32[5,1,192]{2,1,0:T(1,128)} %constant.2.clone.key_ref) | copy-start | bytes 11524
where the time goes:
time: 134 us; the launch traced here: 131 us
  Pallas kernels  124 us (93%)
  local copies, waits for them, and re-layouts  7.16 us (5%)
    pallas_call x1, Pallas kernels, contract(): pl.pallas_call(functools.partial(contract_kernel, workers), out_shape=jax...  122 us
    unnamed x17, local copies, waits for them, and re-layouts  7.16 us

commit v1 on v0

v1 whole, which is shorter than its diff:
```python
import functools

import jax
import jax.numpy as jnp
import numpy as np
from jax import lax
from jax.experimental import pallas as pl
from jax.experimental.pallas import tpu as pltpu
from jax.sharding import PartitionSpec as P

MOST = 6
LEGS = 3
PAD = 8
MESH = pl.DeviceIdType.MESH


def plan(workers, own_a):
    half, quarter = workers // 2, workers // 4
    near, mid_j = own_a // 2, own_a // 2
    low_far = half * own_a
    low_late = low_far + quarter * own_a
    last = mid_j + (own_a - mid_j) // 2
    chunks = []

    def add(kind, low, js):
        if len(js) > 0:
            chunks.append((kind, low + quarter * js[0], quarter * len(js), tuple(js)))
            events.append(("work", len(chunks) - 1))

    events = []
    for c in range(2):
        chunks.append(("near", c * half * near, half * near, (c,)))
    events.append(("work", 0))
    events += [("late", j) for j in range(mid_j)]
    events.append(("work", 1))
    events += [("far", j) for j in range(mid_j - 1)]
    add("late", low_late, list(range(mid_j)))
    events += [("far", j) for j in range(mid_j - 1, mid_j + 1)]
    add("far", low_far, list(range(mid_j)))
    events += [("far", j) for j in range(mid_j + 1, own_a)]
    add("far", low_far, list(range(mid_j, own_a)))
    events += [("late", j) for j in range(mid_j, last)]
    add("late", low_late, list(range(mid_j, last)))
    events += [("late", j) for j in range(last, own_a)]
    add("late", low_late, list(range(last, own_a)))

    most = max(count for _, _, count, _ in chunks)
    keys = np.full((2, len(chunks), 1, MOST * most), -1)
    for side in range(2):
        for c, (kind, _, count, js) in enumerate(chunks):
            at = np.arange(count)
            if kind == "near":
                v = side * half + at // near
                j = js[0] * near + at % near
            else:
                sub = 1 - side if kind == "far" else side
                v = (1 - side) * half + sub * quarter + at % quarter
                j = js[0] + at // quarter
            for d in range(MOST):
                keys[side, c, 0, d * count : (d + 1) * count] = d * (workers * own_a) + v * own_a + j
    return chunks, events, most, keys


def contract_kernel(
    workers,
    slots,
    ids_ref,
    pids_ref,
    counts_ref,
    weights_ref,
    key_ref,
    x_hbm,
    p_hbm,
    o_ref,
    xs,
    pv,
    rows,
    xnear,
    xfar,
    lnear,
    lgate,
    lgate_late,
    lfwd,
    xall,
    lbuf,
    fwd,
    legs,
    p1s,
    p2s,
    p3s,
    mid,
    acc,
    stage,
    first_ref,
    rank_ref,
    slot_ref,
    start_ref,
    in_sem,
    lsend,
    lrecv,
    msend,
    mrecv,
    gsend,
    grecv,
    nsend,
    nrecv,
    csend,
    crecv,
    fsend,
    frecv,
    *gates,
):
    own_a, extent = xs.shape[1], xs.shape[3]
    own_rows = lbuf.shape[2]
    diagrams = weights_ref.shape[0]
    half, quarter = workers // 2, workers // 4
    near = own_a // 2
    chunks, events, most, _ = plan(workers, own_a)
    kinds = ("far", "late")
    gate = {"far": gates[:own_a], "late": gates[own_a:]}
    leg_gate = {"far": lgate, "late": lgate_late}
    low_of = {"far": half * own_a, "late": (half + quarter) * own_a}
    step = extent + PAD
    me = lax.axis_index("work")
    side = lax.div(me, half)
    own = lax.rem(me, half)
    lane = lax.rem(me, quarter)
    sub = lax.div(own, quarter)
    base = side * half
    other = (1 - side) * half
    is_gate = sub == 1 - side
    far_gate = lane + quarter * (2 - side)
    owner = {"far": other + (1 - side) * quarter, "late": other + side * quarter}

    p_copy = pltpu.make_async_copy(p_hbm, pv, in_sem.at[0])
    x_copy = pltpu.make_async_copy(x_hbm, xs, in_sem.at[1])
    p_copy.start()
    x_copy.start()

    barrier = pltpu.get_barrier_semaphore()

    def greet(peer):
        pl.semaphore_signal(barrier, inc=1, device_id={"work": peer}, device_id_type=MESH)

    @pl.loop(1, half)
    def _(t):
        greet(base + lax.rem(own + t, half))

    for part in range(2):
        greet(other + part * quarter + lane)

    def tables(low, with_slots):
        def ranked(s, count):
            v = ids_ref[low + s]
            first = lax.fori_loop(
                0,
                half,
                lambda k, m: jnp.minimum(m, jnp.where(ids_ref[low + k] == v, k, half)),
                jnp.int32(half),
                unroll=True,
            )
            is_first = first == s
            first_ref[s] = jnp.where(is_first, count, -1)
            rank_ref[s] = count
            if with_slots:
                slot_ref[s] = rank_ref[first]
            return count + jnp.where(is_first, 1, 0)

        lax.fori_loop(0, half, ranked, jnp.int32(0))

    def start_of(s, start):
        start_ref[s] = start
        return start + counts_ref[s]

    lax.fori_loop(0, workers, start_of, jnp.int32(0))

    def pick_legs(s, source, store):
        for slot in range(MOST):
            d = jnp.minimum(start_ref[base + s] + slot, diagrams - 1)
            for leg in range(LEGS):
                store(slot * LEGS + leg, source[pids_ref[leg, d]])

    def near_leg_copy(t):
        to = lax.rem(own + t, half)
        return pltpu.make_async_remote_copy(
            src_ref=lnear.at[to],
            dst_ref=lbuf.at[me],
            send_sem=lsend.at[t],
            recv_sem=lrecv.at[t],
            device_id={"work": base + to},
            device_id_type=MESH,
        )

    def far_leg_copy(kind):
        return pltpu.make_async_remote_copy(
            src_ref=rows,
            dst_ref=leg_gate[kind],
            send_sem=msend.at[0],
            recv_sem=mrecv.at[kinds.index(kind)],
            device_id={"work": far_gate},
            device_id_type=MESH,
        )

    def pass_leg_copy(kind, t):
        part = kinds.index(kind)
        to = lax.rem(own + t, half)
        return pltpu.make_async_remote_copy(
            src_ref=lfwd.at[part, to],
            dst_ref=lbuf.at[owner[kind] + lane],
            send_sem=gsend.at[part, t],
            recv_sem=grecv.at[part, lane],
            device_id={"work": base + to},
            device_id_type=MESH,
        )

    def leg_arrival(kind, via):
        part = kinds.index(kind)
        return pltpu.make_async_remote_copy(
            src_ref=lfwd.at[part, 0],
            dst_ref=lbuf.at[owner[kind] + via],
            send_sem=gsend.at[part, 0],
            recv_sem=grecv.at[part, via],
            device_id={"work": far_gate},
            device_id_type=MESH,
        )

    def near_copy(c, t):
        to = lax.rem(own + t, half)
        return pltpu.make_async_remote_copy(
            src_ref=xnear.at[to, pl.ds(c * near, near)],
            dst_ref=xall.at[pl.ds((c * half + own) * near, near)],
            send_sem=nsend.at[c, t],
            recv_sem=nrecv.at[c, t],
            device_id={"work": base + to},
            device_id_type=MESH,
        )

    def far_copy(kind, j):
        return pltpu.make_async_remote_copy(
            src_ref=xfar.at[j],
            dst_ref=gate[kind][j],
            send_sem=csend.at[j],
            recv_sem=crecv.at[kinds.index(kind), j],
            device_id={"work": far_gate},
            device_id_type=MESH,
        )

    def pass_copy(kind, j, t):
        part = kinds.index(kind)
        to = lax.rem(own + t, half)
        return pltpu.make_async_remote_copy(
            src_ref=fwd.at[part, j, to],
            dst_ref=xall.at[low_of[kind] + j * quarter + lane],
            send_sem=fsend.at[part, j, t],
            recv_sem=frecv.at[part, j, lane],
            device_id={"work": base + to},
            device_id_type=MESH,
        )

    def arrival(kind, j, via):
        part = kinds.index(kind)
        return pltpu.make_async_remote_copy(
            src_ref=fwd.at[part, j, 0],
            dst_ref=xall.at[low_of[kind] + j * quarter + via],
            send_sem=fsend.at[part, j, 0],
            recv_sem=frecv.at[part, j, via],
            device_id={"work": far_gate},
            device_id_type=MESH,
        )

    def by_role(make):
        pl.when(is_gate)(make("late").start)
        pl.when(jnp.logical_not(is_gate))(make("far").start)

    p_copy.wait()
    for r in range(own_rows):
        rows[:, r, :] = pv[:, r * extent : (r + 1) * extent]
    tables(other, False)

    pl.semaphore_wait(barrier, half + 1)
    by_role(far_leg_copy)

    @pl.loop(0, half)
    def _(s):
        def store(m, value):
            lnear[s, m] = value

        pick_legs(s, rows, store)

    @pl.loop(1, half)
    def _(t):
        near_leg_copy(t).start()

    x_copy.wait()

    @pl.loop(0, half)
    def _(s):
        for j in range(own_a):
            xnear[s, j] = xs[ids_ref[base + s], j]

    for c in range(2):

        @pl.loop(1, half)
        def _(t):
            near_copy(c, t).start()

    @pl.loop(0, slots)
    def _(k):
        source = lax.fori_loop(
            0,
            half,
            lambda s, v: v + jnp.where(first_ref[s] == k, ids_ref[other + s], 0),
            jnp.int32(0),
            unroll=True,
        )
        for j in range(own_a):
            xfar[j, k] = xs[source, j]

    for j in range(own_a):
        by_role(functools.partial(far_copy, j=j))

    lbuf[me] = lnear[own]
    for c in range(2):
        for j in range(near):
            xall[(c * half + own) * near + j] = xnear[own, c * near + j]

    tables(base, True)

    factors = []
    for d in range(MOST):
        value = weights_ref[jnp.minimum(start_ref[me] + d, diagrams - 1)]
        factors.append(jnp.where(d < counts_ref[me], value, 0.0))

    @pl.when(is_gate)
    def _():
        for part, kind in enumerate(kinds):
            far_leg_copy(kind).wait_recv()

            @pl.loop(0, half)
            def _(s):
                def store(m, value):
                    lfwd[part, s, m] = value

                pick_legs(s, leg_gate[kind], store)

            lbuf[owner[kind] + lane] = lfwd[part, own]

            @pl.loop(1, half)
            def _(t):
                pass_leg_copy(kind, t).start()

    def unless_own(via, act):
        pl.when(jnp.logical_not(jnp.logical_and(is_gate, via == lane)))(act)

    @pl.loop(1, half)
    def _(t):
        near_leg_copy(t).wait_recv()

    for kind in kinds:

        @pl.loop(0, quarter)
        def _(via):
            unless_own(via, leg_arrival(kind, via).wait_recv)

    @pl.loop(0, MOST * LEGS)
    def _(m):
        for v in range(workers):
            legs[m, v * own_rows : (v + 1) * own_rows, :] = lbuf[v, m].astype(jnp.float32)

    firsts = []
    for d in range(MOST):
        firsts.append(legs[LEGS * d].astype(jnp.bfloat16))
        p2s[d * extent : (d + 1) * extent, :] = legs[LEGS * d + 1].astype(jnp.bfloat16)
        p3s[d] = legs[LEGS * d + 2].T.astype(jnp.bfloat16)
    wall = jnp.concatenate(firsts, axis=1)
    for c, (_, _, count, _) in enumerate(chunks):
        width = MOST * count
        at = lax.broadcasted_iota(jnp.int32, (MOST * extent, width), 0)
        chosen = jnp.where(at == key_ref[side, c, :, :width], 1.0, 0.0).astype(jnp.bfloat16)
        p1s[c, :, :width] = jnp.dot(wall, chosen, preferred_element_type=jnp.float32).astype(
            jnp.bfloat16
        )

    def forward(kind, j):
        part = kinds.index(kind)

        @pl.when(is_gate)
        def _():
            far_copy(kind, j).wait_recv()

            @pl.loop(0, half)
            def _(s):
                fwd[part, j, s] = gate[kind][j][slot_ref[s]]

            xall[low_of[kind] + j * quarter + lane] = fwd[part, j, own]

            @pl.loop(1, half)
            def _(t):
                pass_copy(kind, j, t).start()

    group = 4
    wide = 8

    def work(c):
        kind, low, count, js = chunks[c]
        if kind == "near":

            @pl.loop(1, half)
            def _(t):
                near_copy(js[0], t).wait_recv()

        else:
            for j in js:

                @pl.loop(0, quarter)
                def _(via):
                    unless_own(via, arrival(kind, j, via).wait_recv)

        @pl.loop(0, count // group, unroll=2)
        def _(g):
            both = jnp.concatenate([xall[low + g * group + i] for i in range(group)], axis=1)
            for d in range(MOST):
                z = jnp.dot(
                    p2s[d * extent : (d + 1) * extent, :], both, preferred_element_type=jnp.float32
                ).astype(jnp.bfloat16)
                stacked = jnp.concatenate(
                    [z[:, i * extent : (i + 1) * extent] for i in range(group)], axis=0
                )
                y = jnp.dot(stacked, p3s[d], preferred_element_type=jnp.float32) * factors[d]
                for i in range(group):
                    at = pl.multiple_of((d * count + group * g + i) * step, 8)
                    mid[pl.ds(at, extent), :] = y[i * extent : (i + 1) * extent]

        def pieces(b):
            cols = [
                mid[pl.ds(wide * b + h, MOST * count, stride=step), :].astype(jnp.bfloat16)
                for h in range(wide)
            ]
            t = jnp.dot(
                p1s[c, :, : MOST * count],
                jnp.concatenate(cols, axis=1),
                preferred_element_type=jnp.float32,
            )
            out = []
            for h in range(wide):
                at = pl.ds(pl.multiple_of((wide * b + h) * extent, 8), extent)
                piece = t[:, h * extent : (h + 1) * extent]
                out.append((at, piece if c == 0 else piece + acc[at, :]))
            return out

        if c < len(chunks) - 1:

            @pl.loop(0, extent // wide)
            def _(b):
                for at, piece in pieces(b):
                    acc[at, :] = piece

        else:

            @pl.loop(0, extent // (2 * wide))
            def _(b):
                for part in range(2):
                    for h, (at, piece) in enumerate(pieces(2 * b + part)):
                        stage[:, part * wide + h, :] = piece
                at = pl.ds(pl.multiple_of(2 * wide * b, 2 * wide), 2 * wide)
                o_ref[:, at, :] = stage[:, : 2 * wide, :].astype(jnp.bfloat16)

    for what, at in events:
        if what == "work":
            work(at)
        else:
            forward(what, at)

    @pl.loop(1, half)
    def _(t):
        near_leg_copy(t).wait_send()

    far_leg_copy("far").wait_send()
    for c in range(2):

        @pl.loop(1, half)
        def _(t):
            near_copy(c, t).wait_send()

    for j in range(own_a):
        far_copy("far", j).wait_send()

    @pl.when(is_gate)
    def _():
        for kind in kinds:

            @pl.loop(1, half)
            def _(t):
                pass_leg_copy(kind, t).wait_send()

            for j in range(own_a):

                @pl.loop(1, half)
                def _(t):
                    pass_copy(kind, j, t).wait_send()


def contract(x, perambs, ids, pids, counts, weights, workers, slots):
    own_a, extent = x.shape[1], x.shape[2]
    own_rows = own_a
    half, quarter = workers // 2, workers // 4
    chunks, _, most, keys = plan(workers, own_a)
    step = extent + PAD
    smem = pl.BlockSpec(memory_space=pltpu.SMEM)
    hbm = pl.BlockSpec(memory_space=pltpu.HBM)
    slab = (extent, extent)
    bf16, f32 = jnp.bfloat16, jnp.float32
    legs = MOST * LEGS
    pieces = (perambs.shape[0], own_rows, extent)
    dma = pltpu.SemaphoreType.DMA
    return pl.pallas_call(
        functools.partial(contract_kernel, workers, slots),
        out_shape=jax.ShapeDtypeStruct((extent, extent, extent), bf16),
        in_specs=[smem, smem, smem, smem, pl.BlockSpec(memory_space=pltpu.VMEM), hbm, hbm],
        out_specs=pl.BlockSpec(memory_space=pltpu.VMEM),
        scratch_shapes=[
            pltpu.VMEM(x.shape, bf16),
            pltpu.VMEM(perambs.shape, bf16),
            pltpu.VMEM(pieces, bf16),
            pltpu.VMEM((half, own_a) + slab, bf16),
            pltpu.VMEM((own_a, slots) + slab, bf16),
            pltpu.VMEM((half, legs, own_rows, extent), bf16),
            pltpu.VMEM(pieces, bf16),
            pltpu.VMEM(pieces, bf16),
            pltpu.VMEM((2, half, legs, own_rows, extent), bf16),
            pltpu.VMEM((workers * own_a,) + slab, bf16),
            pltpu.VMEM((workers, legs, own_rows, extent), bf16),
            pltpu.VMEM((2, own_a, half) + slab, bf16),
            pltpu.VMEM((legs,) + slab, f32),
            pltpu.VMEM((len(chunks), extent, MOST * most), bf16),
            pltpu.VMEM((MOST * extent, extent), bf16),
            pltpu.VMEM((MOST,) + slab, bf16),
            pltpu.VMEM((MOST * most * step, extent), f32),
            pltpu.VMEM((extent * extent, extent), f32),
            pltpu.VMEM((extent, 24, extent), f32),
            pltpu.SMEM((half,), jnp.int32),
            pltpu.SMEM((half,), jnp.int32),
            pltpu.SMEM((half,), jnp.int32),
            pltpu.SMEM((workers,), jnp.int32),
            dma((2,)),
            dma((half,)),
            dma((half,)),
            dma((1,)),
            dma((2,)),
            dma((2, half)),
            dma((2, quarter)),
            dma((2, half)),
            dma((2, half)),
            dma((own_a,)),
            dma((2, own_a)),
            dma((2, own_a, half)),
            dma((2, own_a, quarter)),
        ]
        + [pltpu.VMEM((slots,) + slab, bf16) for _ in range(2 * own_a)],
        compiler_params=pltpu.CompilerParams(
            vmem_limit_bytes=54 * 1024 * 1024, collective_id=0, has_side_effects=True
        ),
        name="contract",
    )(ids, pids, counts, weights, jnp.asarray(keys, jnp.int32), x, perambs)


def per_device(sources, perambs, source_ids, peramb_ids, sink_counts, weights):
    workers = lax.axis_size("work")
    extent = sources.shape[2]
    own_a = sources.shape[1] // extent
    x = sources.reshape(-1, own_a, extent, extent)
    total = contract(
        x, perambs, source_ids, peramb_ids.T, sink_counts, weights, workers, workers // 2
    )
    return total.reshape(1, extent * extent, extent)


def solution(mesh):
    return jax.shard_map(
        per_device,
        mesh=mesh,
        in_specs=(P("cfg", "work", None), P("cfg", "work"), P(), P(), P(), P()),
        out_specs=P(("cfg", "work"), None, None),
        check_vma=False,
    )
```

time: 134 us -> 153 us (1.14); the launches traced: 131 us -> 152 us
  Pallas kernels: 124 us -> 149 us
  local copies, waits for them, and re-layouts: 7.16 us -> 3.74 us
    pallas_call x2 -> x1, Pallas kernels: 124 us -> 149 us  [contract(): pl.pallas_call(functools.partial(contract_kernel, workers, slots), out_sh...]
    unnamed x17 -> x1, local copies, waits for them, and re-layouts: 7.16 us -> 3.74 us
where the time goes in v1:
time: 153 us; the launch traced here: 152 us
  Pallas kernels  149 us (97%)
  local copies, waits for them, and re-layouts  3.74 us (2%)
    pallas_call x1, Pallas kernels, contract(): pl.pallas_call(functools.partial(contract_kernel, workers, slots), out_sh...  149 us
    unnamed x1, local copies, waits for them, and re-layouts  3.74 us

profile of v1, /device:TPU:0, one launch (start us, length us, event | category | flops | bytes accessed | tf_op | source)
XLA Modules:
  0.0 152.4 jit_solution(9025398979683606153)
XLA Ops:
  0.0 148.6 %contract.1 = bf16[128,128,128]{2,1,0:T(8,128)(2,1)} custom-call(s32[16]{0:T(128)} %ids_ref.1, s32[3,48]{1,0:T(4,128)} %bitcast.5, s32[16]{0:T(128)} %counts_ref.1, f32[48]{0:T(128)} %weights_ref.1, s32[2,7,1,192]{3,2,1,0:T(1,128)} %constant.2.clone.key_ref, bf16[16,8,128,128]{3,2,1,0:T(8,128)(2,1)} %bitcast.4, bf16[96,1024]{1,0:T(8,128)(2,1)} %p_hbm.1), custom_call_target="tpu_custom_call" | custom-call | tf_op jit(solution)/shard_map/contract/pallas_call | solution.py:516
  148.6 3.7 %copy.9 = bf16[1,16384,128]{2,1,0:T(8,128)(2,1)} copy(bf16[1,16384,128]{2,1,0:T(8,128)(2,1)} %bitcast.3) | data formatting | bytes 8388608

commit v2 on v1

--- a/solution.py
+++ b/solution.py
@@ -11,54 +11,61 @@
 MOST = 6
 LEGS = 3
 PAD = 8
+GROUP = 4
+WIDE = 8
 MESH = pl.DeviceIdType.MESH
 
 
-def plan(workers, own_a):
+def plan(workers, own_a, slots):
     half, quarter = workers // 2, workers // 4
-    near, mid_j = own_a // 2, own_a // 2
-    low_far = half * own_a
-    low_late = low_far + quarter * own_a
-    last = mid_j + (own_a - mid_j) // 2
-    chunks = []
-
-    def add(kind, low, js):
-        if len(js) > 0:
-            chunks.append((kind, low + quarter * js[0], quarter * len(js), tuple(js)))
-            events.append(("work", len(chunks) - 1))
-
-    events = []
+    near = own_a // 2
+    size = half * near
+    early = max(0, min(own_a - 2, int(quarter * own_a / slots - 0.75)))
+    items = [("late", j) for j in range(early)]
+    items += [("far", j) for j in range(own_a)]
+    items += [("late", j) for j in range(early, own_a)]
+    tail = max(1, 8 // quarter)
+    body = len(items) - tail
+
+    slabs = []
     for c in range(2):
-        chunks.append(("near", c * half * near, half * near, (c,)))
-    events.append(("work", 0))
-    events += [("late", j) for j in range(mid_j)]
-    events.append(("work", 1))
-    events += [("far", j) for j in range(mid_j - 1)]
-    add("late", low_late, list(range(mid_j)))
-    events += [("far", j) for j in range(mid_j - 1, mid_j + 1)]
-    add("far", low_far, list(range(mid_j)))
-    events += [("far", j) for j in range(mid_j + 1, own_a)]
-    add("far", low_far, list(range(mid_j, own_a)))
-    events += [("late", j) for j in range(mid_j, last)]
-    add("late", low_late, list(range(mid_j, last)))
-    events += [("late", j) for j in range(last, own_a)]
-    add("late", low_late, list(range(last, own_a)))
-
-    most = max(count for _, _, count, _ in chunks)
-    keys = np.full((2, len(chunks), 1, MOST * most), -1)
+        slabs += [(("near", v), c * near + j) for v in range(half) for j in range(near)]
+    for kind, j in items:
+        slabs += [((kind, v), j) for v in range(quarter)]
+    split = 2 * size + body * quarter
+    groups = [slabs[low : min(low + size, split)] for low in range(0, split, size)]
+    groups.append(slabs[split:])
+    keys = np.full((2, len(groups), 1, MOST * size), -1)
     for side in range(2):
-        for c, (kind, _, count, js) in enumerate(chunks):
-            at = np.arange(count)
-            if kind == "near":
-                v = side * half + at // near
-                j = js[0] * near + at % near
-            else:
-                sub = 1 - side if kind == "far" else side
-                v = (1 - side) * half + sub * quarter + at % quarter
-                j = js[0] + at // quarter
-            for d in range(MOST):
-                keys[side, c, 0, d * count : (d + 1) * count] = d * (workers * own_a) + v * own_a + j
-    return chunks, events, most, keys
+        first = {
+            "near": side * half,
+            "far": (1 - side) * half + (1 - side) * quarter,
+            "late": (1 - side) * half + side * quarter,
+        }
+        for g, group in enumerate(groups):
+            stride = size if g < len(groups) - 1 else len(group)
+            for at, ((kind, v), j) in enumerate(group):
+                for d in range(MOST):
+                    a = (first[kind] + v) * own_a + j
+                    keys[side, g, 0, d * stride + at] = d * (workers * own_a) + a
+
+    unit = GROUP
+    near_steps, item_steps = size // unit, quarter // unit
+    begin = 2 * near_steps
+    when = []
+    for f in range(len(items)):
+        if f < 3:
+            at = (0, near_steps - 1, near_steps)[f]
+        elif f == 3 and early > 3:
+            at = begin - 1
+        elif f < body:
+            at = begin + item_steps * (f - 2)
+        elif f < len(items) - 1:
+            at = begin + item_steps * (f - 1)
+        else:
+            at = begin + item_steps * body
+        when.append(min(at, begin + item_steps * f))
+    return items, early, size, len(groups), body, when, keys
 
 
 def contract_kernel(
@@ -115,7 +122,7 @@
     diagrams = weights_ref.shape[0]
     half, quarter = workers // 2, workers // 4
     near = own_a // 2
-    chunks, events, most, _ = plan(workers, own_a)
+    items, early, size, groups, main, when, _ = plan(workers, own_a, slots)
     kinds = ("far", "late")
     gate = {"far": gates[:own_a], "late": gates[own_a:]}
     leg_gate = {"far": lgate, "late": lgate_late}
@@ -257,17 +264,6 @@
             device_id_type=MESH,
         )
 
-    def arrival(kind, j, via):
-        part = kinds.index(kind)
-        return pltpu.make_async_remote_copy(
-            src_ref=fwd.at[part, j, 0],
-            dst_ref=xall.at[low_of[kind] + j * quarter + via],
-            send_sem=fsend.at[part, j, 0],
-            recv_sem=frecv.at[part, j, via],
-            device_id={"work": far_gate},
-            device_id_type=MESH,
-        )
-
     def by_role(make):
         pl.when(is_gate)(make("late").start)
         pl.when(jnp.logical_not(is_gate))(make("far").start)
@@ -298,11 +294,13 @@
         for j in range(own_a):
             xnear[s, j] = xs[ids_ref[base + s], j]
 
-    for c in range(2):
-
+    def start_near(c):
         @pl.loop(1, half)
         def _(t):
             near_copy(c, t).start()
+
+    start_near(0)
+    pl.when(jnp.logical_not(is_gate))(lambda: start_near(1))
 
     @pl.loop(0, slots)
     def _(k):
@@ -319,35 +317,43 @@
     for j in range(own_a):
         by_role(functools.partial(far_copy, j=j))
 
+    @pl.when(is_gate)
+    def _():
+        for part, kind in enumerate(kinds):
+            far_leg_copy(kind).wait_recv()
+
+            @pl.loop(0, half)
+            def _(s):
+                def store(m, value):
+                    lfwd[part, s, m] = value
+
+                pick_legs(s, leg_gate[kind], store)
+
+            lbuf[owner[kind] + lane] = lfwd[part, own]
+
+            @pl.loop(1, half)
+            def _(t):
+                pass_leg_copy(kind, t).start()
+
+        start_near(1)
+
+    tables(base, True)
+
+    @pl.loop(0, extent)
+    def _(b):
+        acc[pl.ds(pl.multiple_of(b * extent, extent), extent), :] = jnp.zeros(
+            (extent, extent), jnp.float32
+        )
+
     lbuf[me] = lnear[own]
     for c in range(2):
         for j in range(near):
             xall[(c * half + own) * near + j] = xnear[own, c * near + j]
 
-    tables(base, True)
-
     factors = []
     for d in range(MOST):
         value = weights_ref[jnp.minimum(start_ref[me] + d, diagrams - 1)]
         factors.append(jnp.where(d < counts_ref[me], value, 0.0))
-
-    @pl.when(is_gate)
-    def _():
-        for part, kind in enumerate(kinds):
-            far_leg_copy(kind).wait_recv()
-
-            @pl.loop(0, half)
-            def _(s):
-                def store(m, value):
-                    lfwd[part, s, m] = value
-
-                pick_legs(s, leg_gate[kind], store)
-
-            lbuf[owner[kind] + lane] = lfwd[part, own]
-
-            @pl.loop(1, half)
-            def _(t):
-                pass_leg_copy(kind, t).start()
 
     def unless_own(via, act):
         pl.when(jnp.logical_not(jnp.logical_and(is_gate, via == lane)))(act)
@@ -373,13 +379,11 @@
         p2s[d * extent : (d + 1) * extent, :] = legs[LEGS * d + 1].astype(jnp.bfloat16)
         p3s[d] = legs[LEGS * d + 2].T.astype(jnp.bfloat16)
     wall = jnp.concatenate(firsts, axis=1)
-    for c, (_, _, count, _) in enumerate(chunks):
-        width = MOST * count
-        at = lax.broadcasted_iota(jnp.int32, (MOST * extent, width), 0)
-        chosen = jnp.where(at == key_ref[side, c, :, :width], 1.0, 0.0).astype(jnp.bfloat16)
-        p1s[c, :, :width] = jnp.dot(wall, chosen, preferred_element_type=jnp.float32).astype(
-            jnp.bfloat16
-        )
+    width = MOST * size
+    at = lax.broadcasted_iota(jnp.int32, (MOST * extent, width), 0)
+    for g in range(groups):
+        chosen = jnp.where(at == key_ref[side, g], 1.0, 0.0).astype(jnp.bfloat16)
+        p1s[g] = jnp.dot(wall, chosen, preferred_element_type=jnp.float32).astype(jnp.bfloat16)
 
     def forward(kind, j):
         part = kinds.index(kind)
@@ -398,78 +402,101 @@
             def _(t):
                 pass_copy(kind, j, t).start()
 
-    group = 4
-    wide = 8
-
-    def work(c):
-        kind, low, count, js = chunks[c]
-        if kind == "near":
-
-            @pl.loop(1, half)
-            def _(t):
-                near_copy(js[0], t).wait_recv()
-
-        else:
-            for j in js:
-
-                @pl.loop(0, quarter)
-                def _(via):
-                    unless_own(via, arrival(kind, j, via).wait_recv)
-
-        @pl.loop(0, count // group, unroll=2)
-        def _(g):
-            both = jnp.concatenate([xall[low + g * group + i] for i in range(group)], axis=1)
-            for d in range(MOST):
-                z = jnp.dot(
-                    p2s[d * extent : (d + 1) * extent, :], both, preferred_element_type=jnp.float32
-                ).astype(jnp.bfloat16)
-                stacked = jnp.concatenate(
-                    [z[:, i * extent : (i + 1) * extent] for i in range(group)], axis=0
-                )
-                y = jnp.dot(stacked, p3s[d], preferred_element_type=jnp.float32) * factors[d]
-                for i in range(group):
-                    at = pl.multiple_of((d * count + group * g + i) * step, 8)
-                    mid[pl.ds(at, extent), :] = y[i * extent : (i + 1) * extent]
-
-        def pieces(b):
-            cols = [
-                mid[pl.ds(wide * b + h, MOST * count, stride=step), :].astype(jnp.bfloat16)
-                for h in range(wide)
-            ]
-            t = jnp.dot(
-                p1s[c, :, : MOST * count],
-                jnp.concatenate(cols, axis=1),
-                preferred_element_type=jnp.float32,
+    near_steps, item_steps = size // GROUP, quarter // GROUP
+    begin = 2 * near_steps
+    main_steps = begin + item_steps * main
+    last_steps = item_steps * (len(items) - main)
+    last = last_steps * GROUP
+
+    def reached(value, limit):
+        span = 2 * workers * own_a
+        return lax.div(value - limit + span, span)
+
+    def pieces(b, columns, count):
+        cols = [
+            mid[pl.ds(WIDE * b + h, MOST * count, stride=step), :].astype(jnp.bfloat16)
+            for h in range(WIDE)
+        ]
+        t = jnp.dot(columns, jnp.concatenate(cols, axis=1), preferred_element_type=jnp.float32)
+        out = []
+        for h in range(WIDE):
+            at = pl.ds(pl.multiple_of((WIDE * b + h) * extent, 8), extent)
+            out.append((at, t[:, h * extent : (h + 1) * extent] + acc[at, :]))
+        return out
+
+    @pl.loop(0, main_steps + last_steps)
+    def _(st):
+        for f, (kind, j) in enumerate(items):
+            pl.when(st == when[f])(functools.partial(forward, kind, j))
+
+        for c in range(2):
+
+            @pl.when(st == c * near_steps)
+            def _():
+                @pl.loop(1, half)
+                def _(t):
+                    near_copy(c, t).wait_recv()
+
+        past = reached(st, begin)
+        i = lax.div(past * (st - begin), item_steps)
+        inside = lax.rem(past * (st - begin), item_steps)
+        middle, end = reached(i, early), reached(i, early + own_a)
+        part = 1 - middle + end
+        j = i - middle * early - end * (own_a - early)
+        low = half * own_a + (part * own_a + j) * quarter
+
+        @pl.when(jnp.logical_and(past == 1, inside == 0))
+        def _():
+            @pl.loop(0, quarter)
+            def _(via):
+                @pl.when(jnp.logical_not(jnp.logical_and(is_gate, via == lane)))
+                def _():
+                    pltpu.make_async_remote_copy(
+                        src_ref=fwd.at[part, j, 0],
+                        dst_ref=xall.at[low + via],
+                        send_sem=fsend.at[part, j, 0],
+                        recv_sem=frecv.at[part, j, via],
+                        device_id={"work": far_gate},
+                        device_id_type=MESH,
+                    ).wait_recv()
+
+        x_at = (1 - past) * st * GROUP + past * (low + inside * GROUP)
+        final = reached(st, main_steps)
+        stride = size + final * (last - size)
+        start = ((1 - final) * lax.rem(st, near_steps) + final * (st - main_steps)) * GROUP
+        both = jnp.concatenate([xall[x_at + n] for n in range(GROUP)], axis=1)
+        for d in range(MOST):
+            z = jnp.dot(
+                p2s[d * extent : (d + 1) * extent, :], both, preferred_element_type=jnp.float32
+            ).astype(jnp.bfloat16)
+            stacked = jnp.concatenate(
+                [z[:, n * extent : (n + 1) * extent] for n in range(GROUP)], axis=0
             )
-            out = []
-            for h in range(wide):
-                at = pl.ds(pl.multiple_of((wide * b + h) * extent, 8), extent)
-                piece = t[:, h * extent : (h + 1) * extent]
-                out.append((at, piece if c == 0 else piece + acc[at, :]))
-            return out
-
-        if c < len(chunks) - 1:
-
-            @pl.loop(0, extent // wide)
+            y = jnp.dot(stacked, p3s[d], preferred_element_type=jnp.float32) * factors[d]
+            for n in range(GROUP):
+                at = pl.multiple_of((d * stride + start + n) * step, 8)
+                mid[pl.ds(at, extent), :] = y[n * extent : (n + 1) * extent]
+
+        full = jnp.logical_and(st < main_steps, lax.rem(st, near_steps) == near_steps - 1)
+
+        @pl.when(jnp.logical_or(full, st == main_steps - 1))
+        def _():
+            g = lax.div(st, near_steps)
+
+            @pl.loop(0, extent // WIDE)
             def _(b):
-                for at, piece in pieces(b):
+                for at, piece in pieces(b, p1s[g], size):
                     acc[at, :] = piece
 
-        else:
-
-            @pl.loop(0, extent // (2 * wide))
-            def _(b):
-                for part in range(2):
-                    for h, (at, piece) in enumerate(pieces(2 * b + part)):
-                        stage[:, part * wide + h, :] = piece
-                at = pl.ds(pl.multiple_of(2 * wide * b, 2 * wide), 2 * wide)
-                o_ref[:, at, :] = stage[:, : 2 * wide, :].astype(jnp.bfloat16)
-
-    for what, at in events:
-        if what == "work":
-            work(at)
-        else:
-            forward(what, at)
+    @pl.loop(0, extent // (2 * WIDE))
+    def _(b):
+        for part in range(2):
+            for h, (at, piece) in enumerate(
+                pieces(2 * b + part, p1s[groups - 1, :, : MOST * last], last)
+            ):
+                stage[:, part * WIDE + h, :] = piece
+        at = pl.ds(pl.multiple_of(2 * WIDE * b, 2 * WIDE), 2 * WIDE)
+        o_ref[:, at, :] = stage[:, : 2 * WIDE, :].astype(jnp.bfloat16)
 
     @pl.loop(1, half)
     def _(t):
@@ -500,11 +527,11 @@
                     pass_copy(kind, j, t).wait_send()
 
 
-def contract(x, perambs, ids, pids, counts, weights, workers, slots):
+def contract(x, perambs, ids, pids, counts, weights, *, workers, slots, number):
     own_a, extent = x.shape[1], x.shape[2]
     own_rows = own_a
     half, quarter = workers // 2, workers // 4
-    chunks, _, most, keys = plan(workers, own_a)
+    _, _, size, groups, _, _, keys = plan(workers, own_a, slots)
     step = extent + PAD
     smem = pl.BlockSpec(memory_space=pltpu.SMEM)
     hbm = pl.BlockSpec(memory_space=pltpu.HBM)
@@ -532,10 +559,10 @@
             pltpu.VMEM((workers, legs, own_rows, extent), bf16),
             pltpu.VMEM((2, own_a, half) + slab, bf16),
             pltpu.VMEM((legs,) + slab, f32),
-            pltpu.VMEM((len(chunks), extent, MOST * most), bf16),
+            pltpu.VMEM((groups, extent, MOST * size), bf16),
             pltpu.VMEM((MOST * extent, extent), bf16),
             pltpu.VMEM((MOST,) + slab, bf16),
-            pltpu.VMEM((MOST * most * step, extent), f32),
+            pltpu.VMEM((MOST * size * step, extent), f32),
             pltpu.VMEM((extent * extent, extent), f32),
             pltpu.VMEM((extent, 24, extent), f32),
             pltpu.SMEM((half,), jnp.int32),
@@ -558,9 +585,9 @@
         ]
         + [pltpu.VMEM((slots,) + slab, bf16) for _ in range(2 * own_a)],
         compiler_params=pltpu.CompilerParams(
-            vmem_limit_bytes=54 * 1024 * 1024, collective_id=0, has_side_effects=True
+            vmem_limit_bytes=48 * 1024 * 1024, collective_id=number, has_side_effects=True
         ),
-        name="contract",
+        name=f"contract_{slots}",
     )(ids, pids, counts, weights, jnp.asarray(keys, jnp.int32), x, perambs)
 
 
@@ -569,8 +596,26 @@
     extent = sources.shape[2]
     own_a = sources.shape[1] // extent
     x = sources.reshape(-1, own_a, extent, extent)
-    total = contract(
-        x, perambs, source_ids, peramb_ids.T, sink_counts, weights, workers, workers // 2
+    half = workers // 2
+    caps = sorted({-(-half * part // 8) for part in (6, 7, 8)})
+    groups = source_ids.reshape(2, half)
+    before = np.tril(np.ones((half, half), bool), -1)
+    same = groups[:, :, None] == groups[:, None, :]
+    repeats = jnp.sum(jnp.any(same & before, axis=2).astype(jnp.int32), axis=1)
+    most = half - jnp.min(repeats)
+    which = sum((most > cap).astype(jnp.int32) for cap in caps[:-1])
+    total = lax.switch(
+        which,
+        [
+            functools.partial(contract, workers=workers, slots=cap, number=i)
+            for i, cap in enumerate(caps)
+        ],
+        x,
+        perambs,
+        source_ids,
+        peramb_ids.T,
+        sink_counts,
+        weights,
     )
     return total.reshape(1, extent * extent, extent)
 

time: 153 us -> 116 us (0.76)
  Pallas kernels: 149 us -> 109 us
  other arithmetic: 0 us -> 1.65 us
    pallas_call x1, Pallas kernels: 149 us -> 109 us  [contract(): pl.pallas_call(functools.partial(contract_kernel, workers, slots), out_sh...]
    unnamed x1, local copies, waits for them, and re-layouts: 3.74 us -> 2.02 us
where the time goes in v2:
time: 116 us; the launch traced here: 115 us
  Pallas kernels  109 us (94%)
  local copies, waits for them, and re-layouts  3.45 us (3%)
  other arithmetic  1.65 us (1%)
    pallas_call x1, Pallas kernels, contract(): pl.pallas_call(functools.partial(contract_kernel, workers, slots), out_sh...  109 us

profile of v2, /device:TPU:0, one launch (start us, length us, event | category | flops | bytes accessed | tf_op | source)
XLA Modules:
  0.0 115.3 jit_solution(4006383845958897529)
XLA Ops:
  0.0 0.7 eq.15
  0.7 0.9 and_reduce_fusion
  1.6 0.1 convert_reduce_fusion
  1.7 0.6 reduce_min.9
  3.0 110.2 %conditional.1 = (bf16[1,16384,128]{2,1,0:T(8,128)(2,1)S(1)}) conditional(s32[]{:T(128)} %clamp.3, (s32[16]{0:T(128)}, s32[3,48]{1,0:T(4,128)}, s32[16]{0:T(128)}, f32[48]{0:T(128)}, bf16[16,8,128,128]{3,2,1,0:T(8,128)(2,1)}, /*index=5*/bf16[96,1024]{1,0:T(8,128)(2,1)}) %tuple.37, (s32[16]{0:T(128)}, ...), branch_computations={%region_3.0_spmd.clone, %region_4.0_spmd.clone, %region_5.0_spmd.c... | conditional | bytes 30756 | solution.py:607
  3.1 0.0 copy-start
  3.1 0.7 copy-done
  3.8 109.2 %contract_7.1 = bf16[128,128,128]{2,1,0:T(8,128)(2,1)S(1)} custom-call(s32[16]{0:T(128)} %get-tuple-element.92.ids_ref, s32[3,48]{1,0:T(4,128)} %get-tuple-element.93.pids_ref, s32[16]{0:T(128)} %get-tuple-element.94.counts_ref, f32[48]{0:T(128)} %get-tuple-element.95.weights_ref, s32[2,5,1,192]{3,2,1,0:T(1,128)S(1)} %copy-done, ...), custom_call_target="tpu_custom_call" | custom-call | tf_op jit(solution)/shard_map/cond/branch_1_fun/contract_7/pallas_call | solution.py:543
  113.2 2.0 %copy.27 = bf16[1,16384,128]{2,1,0:T(8,128)(2,1)} copy(bf16[1,16384,128]{2,1,0:T(8,128)(2,1)S(1)} %get-tuple-element.73) | data formatting | bytes 8388608
Async XLA Ops:
  3.1 0.7 copy-start

commit v3 on v2

--- a/solution.py
+++ b/solution.py
@@ -192,8 +192,8 @@
         return pltpu.make_async_remote_copy(
             src_ref=lnear.at[to],
             dst_ref=lbuf.at[me],
-            send_sem=lsend.at[t],
-            recv_sem=lrecv.at[t],
+            send_sem=lsend.at[0],
+            recv_sem=lrecv.at[0],
             device_id={"work": base + to},
             device_id_type=MESH,
         )
@@ -214,30 +214,26 @@
         return pltpu.make_async_remote_copy(
             src_ref=lfwd.at[part, to],
             dst_ref=lbuf.at[owner[kind] + lane],
-            send_sem=gsend.at[part, t],
-            recv_sem=grecv.at[part, lane],
+            send_sem=gsend.at[0],
+            recv_sem=grecv.at[0],
             device_id={"work": base + to},
             device_id_type=MESH,
         )
 
-    def leg_arrival(kind, via):
-        part = kinds.index(kind)
-        return pltpu.make_async_remote_copy(
-            src_ref=lfwd.at[part, 0],
-            dst_ref=lbuf.at[owner[kind] + via],
-            send_sem=gsend.at[part, 0],
-            recv_sem=grecv.at[part, via],
-            device_id={"work": far_gate},
-            device_id_type=MESH,
-        )
+    def take(ref, sem):
+        pltpu.make_async_copy(ref, ref, sem).wait()
+
+    def take_lanes(ref_of, sem):
+        pl.when(is_gate)(lambda: take(ref_of(quarter - 1), sem))
+        pl.when(jnp.logical_not(is_gate))(lambda: take(ref_of(quarter), sem))
 
     def near_copy(c, t):
         to = lax.rem(own + t, half)
         return pltpu.make_async_remote_copy(
             src_ref=xnear.at[to, pl.ds(c * near, near)],
             dst_ref=xall.at[pl.ds((c * half + own) * near, near)],
-            send_sem=nsend.at[c, t],
-            recv_sem=nrecv.at[c, t],
+            send_sem=nsend.at[0],
+            recv_sem=nrecv.at[c],
             device_id={"work": base + to},
             device_id_type=MESH,
         )
@@ -246,7 +242,7 @@
         return pltpu.make_async_remote_copy(
             src_ref=xfar.at[j],
             dst_ref=gate[kind][j],
-            send_sem=csend.at[j],
+            send_sem=csend.at[0],
             recv_sem=crecv.at[kinds.index(kind), j],
             device_id={"work": far_gate},
             device_id_type=MESH,
@@ -258,8 +254,8 @@
         return pltpu.make_async_remote_copy(
             src_ref=fwd.at[part, j, to],
             dst_ref=xall.at[low_of[kind] + j * quarter + lane],
-            send_sem=fsend.at[part, j, t],
-            recv_sem=frecv.at[part, j, lane],
+            send_sem=fsend.at[0],
+            recv_sem=frecv.at[part, j],
             device_id={"work": base + to},
             device_id_type=MESH,
         )
@@ -355,18 +351,18 @@
         value = weights_ref[jnp.minimum(start_ref[me] + d, diagrams - 1)]
         factors.append(jnp.where(d < counts_ref[me], value, 0.0))
 
-    def unless_own(via, act):
-        pl.when(jnp.logical_not(jnp.logical_and(is_gate, via == lane)))(act)
-
-    @pl.loop(1, half)
-    def _(t):
-        near_leg_copy(t).wait_recv()
-
-    for kind in kinds:
-
-        @pl.loop(0, quarter)
-        def _(via):
-            unless_own(via, leg_arrival(kind, via).wait_recv)
+    lbuf[me] = lnear[own]
+    for c in range(2):
+        for j in range(near):
+            xall[(c * half + own) * near + j] = xnear[own, c * near + j]
+
+    factors = []
+    for d in range(MOST):
+        value = weights_ref[jnp.minimum(start_ref[me] + d, diagrams - 1)]
+        factors.append(jnp.where(d < counts_ref[me], value, 0.0))
+
+    take(lbuf.at[pl.ds(0, half - 1)], lrecv.at[0])
+    take_lanes(lambda lanes: lbuf.at[pl.ds(0, 2 * lanes)], grecv.at[0])
 
     @pl.loop(0, MOST * LEGS)
     def _(m):
@@ -433,9 +429,7 @@
 
             @pl.when(st == c * near_steps)
             def _():
-                @pl.loop(1, half)
-                def _(t):
-                    near_copy(c, t).wait_recv()
+                take(xall.at[pl.ds(0, (half - 1) * near)], nrecv.at[c])
 
         past = reached(st, begin)
         i = lax.div(past * (st - begin), item_steps)
@@ -447,18 +441,7 @@
 
         @pl.when(jnp.logical_and(past == 1, inside == 0))
         def _():
-            @pl.loop(0, quarter)
-            def _(via):
-                @pl.when(jnp.logical_not(jnp.logical_and(is_gate, via == lane)))
-                def _():
-                    pltpu.make_async_remote_copy(
-                        src_ref=fwd.at[part, j, 0],
-                        dst_ref=xall.at[low + via],
-                        send_sem=fsend.at[part, j, 0],
-                        recv_sem=frecv.at[part, j, via],
-                        device_id={"work": far_gate},
-                        device_id_type=MESH,
-                    ).wait_recv()
+            take_lanes(lambda lanes: xall.at[pl.ds(0, lanes)], frecv.at[part, j])
 
         x_at = (1 - past) * st * GROUP + past * (low + inside * GROUP)
         final = reached(st, main_steps)
@@ -498,33 +481,15 @@
         at = pl.ds(pl.multiple_of(2 * WIDE * b, 2 * WIDE), 2 * WIDE)
         o_ref[:, at, :] = stage[:, : 2 * WIDE, :].astype(jnp.bfloat16)
 
-    @pl.loop(1, half)
-    def _(t):
-        near_leg_copy(t).wait_send()
-
+    take(lnear.at[pl.ds(0, half - 1)], lsend.at[0])
     far_leg_copy("far").wait_send()
-    for c in range(2):
-
-        @pl.loop(1, half)
-        def _(t):
-            near_copy(c, t).wait_send()
-
-    for j in range(own_a):
-        far_copy("far", j).wait_send()
+    take(xnear.at[pl.ds(0, half - 1)], nsend.at[0])
+    take(xfar, csend.at[0])
 
     @pl.when(is_gate)
     def _():
-        for kind in kinds:
-
-            @pl.loop(1, half)
-            def _(t):
-                pass_leg_copy(kind, t).wait_send()
-
-            for j in range(own_a):
-
-                @pl.loop(1, half)
-                def _(t):
-                    pass_copy(kind, j, t).wait_send()
+        take(lfwd.at[:, pl.ds(0, half - 1)], gsend.at[0])
+        take(fwd.at[:, :, pl.ds(0, half - 1)], fsend.at[0])
 
 
 def contract(x, perambs, ids, pids, counts, weights, *, workers, slots, number):
@@ -570,18 +535,18 @@
             pltpu.SMEM((half,), jnp.int32),
             pltpu.SMEM((workers,), jnp.int32),
             dma((2,)),
-            dma((half,)),
-            dma((half,)),
+            dma((1,)),
+            dma((1,)),
             dma((1,)),
             dma((2,)),
-            dma((2, half)),
-            dma((2, quarter)),
-            dma((2, half)),
-            dma((2, half)),
-            dma((own_a,)),
+            dma((1,)),
+            dma((1,)),
+            dma((1,)),
+            dma((2,)),
+            dma((1,)),
             dma((2, own_a)),
-            dma((2, own_a, half)),
-            dma((2, own_a, quarter)),
+            dma((1,)),
+            dma((2, own_a)),
         ]
         + [pltpu.VMEM((slots,) + slab, bf16) for _ in range(2 * own_a)],
         compiler_params=pltpu.CompilerParams(
@@ -591,6 +556,41 @@
     )(ids, pids, counts, weights, jnp.asarray(keys, jnp.int32), x, perambs)
 
 
+def choose_kernel(caps, ids_ref, o_ref):
+    half = ids_ref.shape[0] // 2
+
+    def distinct(low):
+        def one(s, count):
+            v = ids_ref[low + s]
+            seen = lax.fori_loop(
+                0,
+                half,
+                lambda k, m: m + jnp.where(jnp.logical_and(k < s, ids_ref[low + k] == v), 1, 0),
+                jnp.int32(0),
+                unroll=True,
+            )
+            return count + jnp.where(seen == 0, 1, 0)
+
+        return lax.fori_loop(0, half, one, jnp.int32(0), unroll=half <= 8)
+
+    most = jnp.maximum(distinct(0), distinct(half))
+    which = jnp.int32(0)
+    for cap in caps[:-1]:
+        which = which + jnp.where(most > cap, 1, 0)
+    o_ref[0] = which
+
+
+def choose(ids, caps):
+    smem = pl.BlockSpec(memory_space=pltpu.SMEM)
+    return pl.pallas_call(
+        functools.partial(choose_kernel, caps),
+        out_shape=jax.ShapeDtypeStruct((1,), jnp.int32),
+        in_specs=[smem],
+        out_specs=smem,
+        name="choose",
+    )(ids)[0]
+
+
 def per_device(sources, perambs, source_ids, peramb_ids, sink_counts, weights):
     workers = lax.axis_size("work")
     extent = sources.shape[2]
@@ -598,12 +598,7 @@
     x = sources.reshape(-1, own_a, extent, extent)
     half = workers // 2
     caps = sorted({-(-half * part // 8) for part in (6, 7, 8)})
-    groups = source_ids.reshape(2, half)
-    before = np.tril(np.ones((half, half), bool), -1)
-    same = groups[:, :, None] == groups[:, None, :]
-    repeats = jnp.sum(jnp.any(same & before, axis=2).astype(jnp.int32), axis=1)
-    most = half - jnp.min(repeats)
-    which = sum((most > cap).astype(jnp.int32) for cap in caps[:-1])
+    which = choose(source_ids, caps)
     total = lax.switch(
         which,
         [

time: 116 us -> 112 us (0.966)
  other arithmetic: 1.65 us -> 0 us
    pallas_call x1, Pallas kernels: 109 us -> 107 us  [contract(): pl.pallas_call(functools.partial(contract_kernel, workers, slots), out_sh...]
    pallas_call x0 -> x1, Pallas kernels: none -> 1.26 us  [choose(): pl.pallas_call(functools.partial(choose_kernel, caps), out_shape=jax.Shap...]
where the time goes in v3:
time: 112 us
  Pallas kernels  108 us (96%)
  local copies, waits for them, and re-layouts  2.71 us (2%)
    pallas_call x1, Pallas kernels, contract(): pl.pallas_call(functools.partial(contract_kernel, workers, slots), out_sh...  107 us

profile of v3, /device:TPU:0, one launch (start us, length us, event | category | flops | bytes accessed | tf_op | source)
XLA Modules:
  0.0 111.5 jit_solution(2120793062929661188)
XLA Ops:
  0.0 1.3 %choose.1 = s32[1]{0:T(128)} custom-call(s32[16]{0:T(128)} %ids_ref.1), custom_call_target="tpu_custom_call" | custom-call | tf_op jit(solution)/shard_map/choose/pallas_call | solution.py:585
  1.9 107.6 %conditional.1 = (bf16[1,16384,128]{2,1,0:T(8,128)(2,1)S(1)}) conditional(s32[]{:T(128)} %bitcast, (s32[16]{0:T(128)}, s32[3,48]{1,0:T(4,128)}, s32[16]{0:T(128)}, f32[48]{0:T(128)}, bf16[16,8,128,128]{3,2,1,0:T(8,128)(2,1)}, /*index=5*/bf16[96,1024]{1,0:T(8,128)(2,1)}) %tuple.37, (s32[16]{0:T(128)}, ...), branch_computations={%region_0.0_spmd.clone, %region_1.0_spmd.clone, %region_2.0_spmd.c... | conditional | bytes 30756 | solution.py:602
  1.9 0.0 copy-start
  2.0 0.7 copy-done
  2.6 106.8 %contract_7.1 = bf16[128,128,128]{2,1,0:T(8,128)(2,1)S(1)} custom-call(s32[16]{0:T(128)} %get-tuple-element.92.ids_ref, s32[3,48]{1,0:T(4,128)} %get-tuple-element.93.pids_ref, s32[16]{0:T(128)} %get-tuple-element.94.counts_ref, f32[48]{0:T(128)} %get-tuple-element.95.weights_ref, s32[2,5,1,192]{3,2,1,0:T(1,128)S(1)} %copy-done, ...), custom_call_target="tpu_custom_call" | custom-call | tf_op jit(solution)/shard_map/cond/branch_1_fun/contract_7/pallas_call | solution.py:508
  109.5 2.0 %copy.26 = bf16[1,16384,128]{2,1,0:T(8,128)(2,1)} copy(bf16[1,16384,128]{2,1,0:T(8,128)(2,1)S(1)} %get-tuple-element.73) | data formatting | bytes 8388608
Async XLA Ops:
  1.9 0.7 copy-start
